TPU v7x, 128 devices: a whole 4x4x4 slice. The times are simulated.
128 devices in a mesh: beam: 16 (over x_lo, y, core), seg: 8 (over z, x_hi).
Axes of the slice: x: 4 (x_hi: 2, x_lo: 2; x = x_hi * 2 + x_lo), y: 4, z: 4, core: 2. Of those that a mesh axis runs over, the one named last changes fastest.
Arguments:
- voltages: bfloat16 [2, 256, 8, 65536], P(None, 'beam', 'seg'), may hold values from -6 to 6
- surv_taps: bfloat16 [32], replicated, may hold values from -1 to 1
- ref_taps: bfloat16 [32], replicated, may hold values from -1 to 1
- tx_owner: int32 [4], replicated, may hold values from 0 to 255
- delay_start: int32 [4], replicated, may hold values from 0 to 384
- doppler_start: int32 [4], replicated, may hold values from 0 to 128
Outputs:
- maps: float32 [4, 256, 128, 128], P(None, 'beam', 'seg')
All inputs are finite; a program needn't handle non-finite values.
Results may differ from a plain program's by a relative error of at most 0.0027.
Values may be sent and summed in bfloat16 or wider, within the bound.
A program may use at most 128 MiB of HBM per device.

v0:
```python
import jax
import jax.numpy as jnp
from jax import lax
from jax.sharding import PartitionSpec as P

TX = 4
DECIM = 4
TAPS = 32
BLOCK_LEN = 64
BLOCKS = 256
DELAYS = 128
DOPPLER = 128
MAXDELAY = 512


def from_root(value, axis, source):
    kept = jnp.where(lax.axis_index(axis) == source, value, 0).astype(value.dtype)
    return lax.psum(kept, axis)


def band_matrix(taps):
    rows = DECIM * BLOCK_LEN + TAPS - 1
    row_ids = jnp.arange(rows, dtype=jnp.int32)[:, None]
    col_ids = jnp.arange(BLOCK_LEN, dtype=jnp.int32)[None, :]
    offset = DECIM * col_ids + TAPS - 1 - row_ids
    tap_ids = jnp.arange(TAPS, dtype=jnp.int32)
    picked = jnp.where(offset[..., None] == tap_ids, taps.astype(jnp.float32), 0.0)
    return jnp.sum(picked, axis=-1).astype(jnp.bfloat16)


def decimate(raw, taps):
    lead = raw.shape[:-1]
    stride = DECIM * BLOCK_LEN
    count = raw.shape[-1] // stride
    blocks = raw.reshape(lead + (count, stride))
    tail = blocks[..., :-1, stride - (TAPS - 1) :]
    tail = jnp.pad(tail, [(0, 0)] * len(lead) + [(1, 0), (0, 0)])
    extended = jnp.concatenate([tail, blocks], axis=-1)
    filtered = jnp.einsum(
        "...k,km->...m", extended, band_matrix(taps), preferred_element_type=jnp.float32
    )
    return filtered.astype(jnp.bfloat16).reshape(lead + (count * BLOCK_LEN,))


def tables(f_lo):
    ells = jnp.arange(BLOCKS, dtype=jnp.int32)
    freqs = f_lo + jnp.arange(DOPPLER, dtype=jnp.int32) - BLOCKS // 2
    phase = ells[:, None] * freqs[None, :] % BLOCKS
    angle = 2.0 * jnp.pi / BLOCKS * phase.astype(jnp.float32)
    return (jnp.cos(angle).astype(jnp.bfloat16), jnp.sin(angle).astype(jnp.bfloat16))


def partial_einsum(form, left, right):
    return jnp.einsum(form, left, right, preferred_element_type=jnp.float32)


def ambiguity(surv, ref, d_lo, f_lo):
    beams = surv.shape[1]
    segs = surv.shape[2]
    span = BLOCK_LEN + DELAYS - 1
    extra = (DELAYS - 1 + BLOCK_LEN - 1) // BLOCK_LEN
    cos_t, sin_t = tables(f_lo)
    scale = BLOCK_LEN ** (-0.5)

    def one_segment(seg):
        blocks_s = lax.dynamic_index_in_dim(surv, seg, 2, keepdims=False).reshape(
            2, beams, BLOCKS, BLOCK_LEN
        )
        ref_seg = lax.dynamic_index_in_dim(ref, seg, 1, keepdims=False)
        rpad = jnp.pad(ref_seg, ((0, 0), (MAXDELAY, extra * BLOCK_LEN)))
        start = MAXDELAY - (DELAYS - 1) - d_lo
        rwin = lax.dynamic_slice_in_dim(rpad, start, (BLOCKS + extra) * BLOCK_LEN, 1)
        rwin = rwin.reshape(2, BLOCKS + extra, BLOCK_LEN)
        window = jnp.concatenate([rwin[:, e : e + BLOCKS] for e in range(extra + 1)], axis=2)[
            ..., :span
        ]
        tiled = jnp.tile(window, (1, 1, BLOCK_LEN + 1))[..., : BLOCK_LEN * (span + 1)]
        toeplitz = tiled.reshape(2, BLOCKS, BLOCK_LEN, span + 1)[..., :DELAYS]
        s_re, s_im = (blocks_s[0], blocks_s[1])
        u_re, u_im = (toeplitz[0], toeplitz[1])
        c_re = (
            partial_einsum("blm,lmi->bli", s_re, u_re) + partial_einsum("blm,lmi->bli", s_im, u_im)
        ) * scale
        c_im = (
            partial_einsum("blm,lmi->bli", s_im, u_re) - partial_einsum("blm,lmi->bli", s_re, u_im)
        ) * scale
        c_re = c_re[..., ::-1].astype(jnp.bfloat16)
        c_im = c_im[..., ::-1].astype(jnp.bfloat16)
        x_re = partial_einsum("blj,lf->bjf", c_re, cos_t) + partial_einsum(
            "blj,lf->bjf", c_im, sin_t
        )
        x_im = partial_einsum("blj,lf->bjf", c_im, cos_t) - partial_einsum(
            "blj,lf->bjf", c_re, sin_t
        )
        return (x_re * x_re + x_im * x_im) * (1.0 / (4 * BLOCKS))

    powers = lax.map(one_segment, jnp.arange(segs, dtype=jnp.int32))
    return jnp.sum(powers, axis=0)


def shards(voltages, surv_taps, ref_taps, tx_owner, delay_start, doppler_start):
    beams_here = voltages.shape[1]
    surv = decimate(voltages, surv_taps)
    segments_all = lax.axis_size("seg") * voltages.shape[2]
    collected = []
    for trans in range(TX):
        owner = tx_owner[trans]
        root = owner // beams_here
        local_beam = owner % beams_here
        mine = lax.dynamic_index_in_dim(voltages, local_beam, 1, keepdims=False)
        arrived = from_root(mine, "beam", root)
        ref = decimate(arrived, ref_taps)
        power = ambiguity(surv, ref, delay_start[trans], doppler_start[trans])
        summed = lax.psum_scatter(power, "seg", scatter_dimension=1, tiled=True)
        collected.append(summed / segments_all)
    return jnp.stack(collected, axis=0)


def solution(mesh):
    return jax.shard_map(
        shards,
        mesh=mesh,
        in_specs=(P(None, "beam", "seg", None), P(), P(), P(), P(), P()),
        out_specs=P(None, "beam", "seg", None),
        check_vma=False,
    )
```

profile of v0, /device:TPU:0, one launch (start us, length us, event | category | flops | bytes accessed | tf_op | source)
XLA Modules:
  0.0 667.7 jit_solution(16479196598512230570)
XLA Ops:
  18.5 11.2 %fusion.80 = (bf16[2,65536]{1,0:T(2,128)(2,1)S(1)}, bf16[2,65536]{1,0:T(2,128)(2,1)S(1)}, bf16[2,65536]{1,0:T(2,128)(2,1)S(1)}, bf16[2,65536]{1,0:T(2,128)(2,1)S(1)}) fusion(pred[]{:T(512)S(6)} %eq.30, bf16[2,16,1,65536]{3,1,2,0:T(8,128)(2,1)} %param.6, s32[]{:T(128)S(6)} %select_n.176, s32[]{:T(128)S(6)} %select_n.186, pred[]{:T(512)S(6)} %eq.34, ...), kind=kLoop, calls=%fused_computation.98 | loop fusion | flops 524288 | bytes 2097172 | tf_op jit(solution)/shard_map/jit(_where)/select_n | solution.py:17
  33.9 5.2 copy.157
  39.0 6.3 copy.97
  64.3 91.9 %all-reduce.12.cloned.1.call-done = (bf16[2,1,256,256]{2,3,0,1:T(8,128)(2,1)}, bf16[2,1,256,256]{2,3,0,1:T(8,128)(2,1)}, bf16[2,1,256,256]{2,3,0,1:T(8,128)(2,1)}, bf16[2,1,256,256]{2,3,0,1:T(8,128)(2,1)}) async-done(((bf16[2,1,256,256]{2,3,0,1:T(8,128)(2,1)}, bf16[2,1,256,256]{2,3,0,1:T(8,128)(2,1)}, bf16[2,1,256,256]{2,3,0,1:T(8,128)(2,1)}, bf16[2,1,256,256]{2,3,0,1:T(8,128)(2,1)}), ...) | async-done | bytes 1048592 | tf_op jit(solution)/shard_map/psum | solution.py:18
  162.3 6.2 tile.62
  168.4 14.5 %tile.63 = bf16[2,256,12415]{1,2,0:T(8,128)(2,1)} reshape(bf16[2,256,65,191]{1,3,2,0:T(8,128)(2,1)} %tile.62) | data formatting | bytes 25425920 | tf_op jit(solution)/shard_map/while/body/eval_jaxpr/tile | solution.py:77
  191.3 6.7 %copy.155 = bf16[1,256,64,128]{3,2,1,0:T(8,128)(2,1)} copy(bf16[1,256,64,128]{1,3,2,0:T(8,128)(2,1)} %get-tuple-element.90) | data formatting | bytes 8388608
  198.0 4.9 fusion.8
  205.5 6.2 tile.60
  211.6 14.5 %tile.61 = bf16[2,256,12415]{1,2,0:T(8,128)(2,1)} reshape(bf16[2,256,65,191]{1,3,2,0:T(8,128)(2,1)} %tile.60) | data formatting | bytes 25425920 | tf_op jit(solution)/shard_map/while/body/eval_jaxpr/tile | solution.py:77
  234.5 6.5 copy.153
  241.0 4.9 fusion.16
  249.8 6.2 tile.58
  255.9 14.5 %tile.59 = bf16[2,256,12415]{1,2,0:T(8,128)(2,1)} reshape(bf16[2,256,65,191]{1,3,2,0:T(8,128)(2,1)} %tile.58) | data formatting | bytes 25425920 | tf_op jit(solution)/shard_map/while/body/eval_jaxpr/tile | solution.py:77
  278.8 6.8 %copy.151 = bf16[1,256,64,128]{3,2,1,0:T(8,128)(2,1)} copy(bf16[1,256,64,128]{1,3,2,0:T(8,128)(2,1)} %get-tuple-element.86) | data formatting | bytes 8388608
  285.6 4.8 fusion.24
  294.3 6.6 copy.154
  300.9 5.6 subtract_bitcast_fusion
  332.8 7.0 %copy.152 = bf16[1,256,64,128]{3,2,1,0:T(8,128)(2,1)} copy(bf16[1,256,64,128]{1,3,2,0:T(8,128)(2,1)} %get-tuple-element.87) | data formatting | bytes 8388608
  339.8 5.5 subtract_bitcast_fusion.1
  360.7 6.6 copy.150
  367.3 5.6 subtract_bitcast_fusion.2
  375.6 6.2 tile.56
  381.8 14.5 %tile.57 = bf16[2,256,12415]{1,2,0:T(8,128)(2,1)} reshape(bf16[2,256,65,191]{1,3,2,0:T(8,128)(2,1)} %tile.56) | data formatting | bytes 25425920 | tf_op jit(solution)/shard_map/while/body/eval_jaxpr/tile | solution.py:77
  416.6 6.7 %copy.149 = bf16[1,256,64,128]{3,2,1,0:T(8,128)(2,1)} copy(bf16[1,256,64,128]{1,3,2,0:T(8,128)(2,1)} %get-tuple-element.84) | data formatting | bytes 8388608
  442.2 6.6 copy.148
  448.7 5.4 subtract_bitcast_fusion.3
  464.3 4.8 fusion.32
  471.9 5.4 add_bitcast_fusion.3
  489.6 19.4 %reduce-scatter.9.cloned.1.call-done = f32[16,16,128]{2,1,0:T(8,128)} async-done(((f32[16,128,128]{2,1,0:T(8,128)}), f32[16,16,128]{2,1,0:T(8,128)}) %reduce-scatter.9.cloned.1.call-update) | async-done | bytes 131088 | tf_op jit(solution)/shard_map/reduce_scatter | solution.py:114
  510.0 74.1 %reduce-scatter.7.cloned.1.call-done = f32[16,16,128]{2,1,0:T(8,128)} async-done(((f32[16,128,128]{2,1,0:T(8,128)}), f32[16,16,128]{2,1,0:T(8,128)}) %reduce-scatter.7.cloned.1.call-update) | async-done | bytes 131088 | tf_op jit(solution)/shard_map/reduce_scatter | solution.py:114
  585.0 74.2 %reduce-scatter.5.cloned.1.call-done = f32[16,16,128]{2,1,0:T(8,128)} async-done(((f32[16,128,128]{2,1,0:T(8,128)}), f32[16,16,128]{2,1,0:T(8,128)}) %reduce-scatter.5.cloned.1.call-update) | async-done | bytes 131088 | tf_op jit(solution)/shard_map/reduce_scatter | solution.py:114
  (182 shorter events, 173.2 us)
Async XLA Ops:
  6.5 149.7 %all-reduce.12.cloned.1.call-start = ((), (), s32[]{:S(2)}) async-start(), calls=%async_computation.8 | async-start | bytes 2097152 | tf_op jit(solution)/shard_map/psum | solution.py:18
  18.4 15.3 %copy-start.21 = (bf16[32]{0:T(256)(128)(2,1)S(1)}, bf16[32]{0:T(256)(128)(2,1)}, u32[]{:S(2)}) copy-start(bf16[32]{0:T(256)(128)(2,1)} %param.7) | copy-start | bytes 196
  18.5 15.3 %copy-start.22 = (bf16[32]{0:T(256)(128)(2,1)S(1)}, bf16[32]{0:T(256)(128)(2,1)}, u32[]{:S(2)}) copy-start(bf16[32]{0:T(256)(128)(2,1)} %param.8) | copy-start | bytes 196
  33.2 455.5 %reduce-scatter.11.cloned.1.call-start = ((), (), s32[]{:S(2)}) async-start(), calls=%async_computation.7 | async-start | bytes 1179648 | tf_op jit(solution)/shard_map/reduce_scatter | solution.py:114
  48.1 3.9 copy-start.14
  52.0 7.5 %copy-start.15 = (s32[4]{0:T(128)S(1)}, s32[4]{0:T(128)}, u32[]{:S(2)}) copy-start(s32[4]{0:T(128)} %param.11) | copy-start | bytes 52
  182.9 4.6 slice-start
  198.0 4.9 copy-start
  226.1 4.6 slice-start.1
  241.0 4.9 copy-start.1
  245.9 2.6 copy-start.20
  270.4 4.6 slice-start.2
  285.6 4.9 copy-start.2
  290.4 2.6 copy-start.19
  300.9 5.6 copy-start.3
  300.9 5.6 copy-start.11
  326.8 3.1 copy-start.8
  332.8 176.3 %reduce-scatter.9.cloned.1.call-start = ((), (), s32[]{:S(2)}) async-start(), calls=%async_computation.6 | async-start | bytes 1179648 | tf_op jit(solution)/shard_map/reduce_scatter | solution.py:114
  339.8 5.5 copy-start.4
  339.8 5.5 copy-start.9
  367.3 5.6 copy-start.5
  367.3 5.6 copy-start.10
  396.3 4.6 slice-start.3
  400.9 3.8 copy-start.12
  416.6 6.7 %copy-start.18 = (s32[128]{0:T(128)S(1)}, s32[128]{0:T(128)}, u32[]{:S(2)}) copy-start(s32[128]{0:T(128)} %add_add_fusion.1) | copy-start | bytes 1540
  423.3 3.2 copy-start.13
  423.3 4.4 copy-start.6
  435.3 148.8 %reduce-scatter.7.cloned.1.call-start = ((), (), s32[]{:S(2)}) async-start(), calls=%async_computation.5 | async-start | bytes 1179648 | tf_op jit(solution)/shard_map/reduce_scatter | solution.py:114
  454.1 4.2 copy-start.17
  458.3 3.1 copy-start.7
  469.1 190.1 %reduce-scatter.5.cloned.1.call-start = ((), (), s32[]{:S(2)}) async-start(), calls=%async_computation.4 | async-start | bytes 1179648 | tf_op jit(solution)/shard_map/reduce_scatter | solution.py:114
  477.3 6.7 %copy-start.16 = (s32[128]{0:T(128)S(1)}, s32[128]{0:T(128)}, u32[]{:S(2)}) copy-start(s32[128]{0:T(128)} %add_add_fusion.3) | copy-start | bytes 1540
Sparse Core Ops, SparseCore 0:
  33.3 122.8 all-reduce.11
  332.9 73.6 reduce-scatter.10
  435.4 73.5 reduce-scatter.8
  512.5 71.5 reduce-scatter.6
  587.5 71.5 reduce-scatter.4
where the time goes:
time: 678 us; the launch traced here: 668 us
  waiting for transfers between devices  260 us (38%)
  local copies, waits for them, and re-layouts  242 us (36%)
  matrix products  96.6 us (14%)
  other arithmetic  39.1 us (6%)
  between operations  29.2 us (4%)
    reduce_scatter x4, waiting for transfers between devices, shards(): summed = lax.psum_scatter(power, 'seg', scatter_dimension=1, tiled=True)  168 us
    psum x1, waiting for transfers between devices, from_root(): return lax.psum(kept, axis)  91.9 us
    dot_general x32, matrix products, partial_einsum(): return jnp.einsum(form, left, right, preferred_element_type=jnp.float32)  89.7 us
    another operation x8, local copies, waits for them, and re-layouts, one_segment(): jnp.tile(window, (1, 1, BLOCK_LEN + 1))[..., :BLOCK_LEN * (span + 1)]  82.7 us
    unnamed x59, local copies, waits for them, and re-layouts  58.7 us
    another operation x8, local copies, waits for them, and re-layouts  33.2 us
    slice x8, local copies, waits for them, and re-layouts, one_segment(): jnp.tile(window, (1, 1, BLOCK_LEN + 1))[..., :BLOCK_LEN * (span + 1)]  18.3 us
    slice x4, local copies, waits for them, and re-layouts, one_segment(): u_re, u_im = (toeplitz[0], toeplitz[1])  15.1 us
  transfers between devices with their start and end apart: 5, of which 4 were waited for; matrix products, arithmetic and copies ran while one was open for 27% of the time, Pallas kernels for 0%

commit v1 on v0

v1 whole, which is shorter than its diff:
```python
import functools

import jax
import jax.numpy as jnp
import numpy as np
from jax import lax
from jax.experimental import pallas as pl
from jax.experimental.pallas import tpu as pltpu
from jax.sharding import PartitionSpec as P

TX = 4
DECIM = 4
TAPS = 32
BLOCK_LEN = 64
BLOCKS = 256
DELAYS = 128
DOPPLER = 128
LANES = 128
BEAMS_HERE = 16
WINDOWS = 128
WINDOWS_STEP = 16
STEPS = WINDOWS // WINDOWS_STEP
RAW_WINDOW = DECIM * LANES
BEAM = 16
SEG = 8
F32 = jnp.float32
BF16 = jnp.bfloat16
MESH = pl.DeviceIdType.MESH


def band_base(taps, backwards):
    rows = lax.broadcasted_iota(jnp.int32, (LANES, LANES), 0)
    cols = lax.broadcasted_iota(jnp.int32, (LANES, LANES), 1)
    if backwards:
        cols = LANES - 1 - cols
    offset = DECIM * cols - rows
    total = jnp.zeros((LANES, LANES), F32)
    for tap in range(TAPS):
        total = jnp.where(offset == tap, taps[tap], total)
    return total


def front_kernel(owner, delay, surv_taps, ref_taps, x, surv, ref, band, halo, picked):
    step = pl.program_id(0)
    me = lax.axis_index("beam")
    lane = lax.broadcasted_iota(jnp.int32, (LANES, LANES), 1)

    @pl.when(step == 0)
    def _():
        forward = band_base(surv_taps, False)
        backward = band_base(ref_taps, True)
        for part in range(5):
            shift = 32 * (part - 1)
            ahead = pltpu.roll(forward, shift % LANES, axis=1)
            behind = pltpu.roll(backward, -shift % LANES, axis=1)
            if part == 0:
                ahead = jnp.where(lane < 8, ahead, 0.0)
                behind = jnp.where(lane >= LANES - 8, behind, 0.0)
            else:
                ahead = jnp.where(lane >= shift, ahead, 0.0)
                behind = jnp.where(lane < LANES - shift, behind, 0.0)
            band[part * LANES : (part + 1) * LANES, :LANES] = ahead.astype(BF16)
            band[part * LANES : (part + 1) * LANES, LANES:] = behind.astype(BF16)
        halo[...] = jnp.zeros_like(halo)
        picked[WINDOWS * 32 :, :] = jnp.zeros((8 * 32, LANES), F32)

    for half in range(2):
        pieces = []
        for w in range(8):
            q = half * 8 + w
            for part in range(2):
                if q == 0:
                    before = halo[part]
                    here = x[part, :, :RAW_WINDOW]
                    pieces.append(jnp.concatenate([before, here], axis=1))
                else:
                    pieces.append(x[part, :, RAW_WINDOW * q - LANES : RAW_WINDOW * (q + 1)])
        left = jnp.concatenate(pieces, axis=0)
        out = jnp.dot(left, band[...], preferred_element_type=F32)
        for w in range(8):
            q = half * 8 + w
            rows = out[w * 32 : (w + 1) * 32]
            surv[q] = rows[:, :LANES].astype(BF16)
            at = pl.multiple_of((WINDOWS - 1 - WINDOWS_STEP * step - q) * 32, 32)
            picked[pl.ds(at, 32), :] = rows[:, LANES:]
    for part in range(2):
        halo[part] = x[part, :, WINDOWS_STEP * RAW_WINDOW - LANES :]

    @pl.when(step == STEPS - 1)
    def _():
        for k in range(TX):
            mine = lax.div(owner[k], BEAMS_HERE) == me
            local = lax.rem(owner[k], BEAMS_HERE)
            whole = lax.div(delay[k], LANES)
            rest = lax.rem(delay[k], LANES)
            turn = lax.rem(LANES - rest, LANES)
            for part in range(2):
                start = whole * 32 + part * BEAMS_HERE + local
                first = picked[pl.ds(start, WINDOWS, stride=32), :]
                second = picked[pl.ds(start + 32, WINDOWS, stride=32), :]
                moved = jnp.where(
                    lane < LANES - rest,
                    pltpu.roll(first, turn, axis=1),
                    pltpu.roll(second, turn, axis=1),
                )
                moved = jnp.where(mine, moved, 0.0).astype(BF16)
                ref[k, part * 8 : (part + 1) * 8] = moved.reshape(8, 16, LANES)


def front(voltages, surv_taps, ref_taps, tx_owner, delay_start):
    smem = pl.BlockSpec(memory_space=pltpu.SMEM)
    x = voltages.reshape(2, BEAMS_HERE, DECIM * WINDOWS * LANES)
    return pl.pallas_call(
        front_kernel,
        grid=(STEPS,),
        in_specs=[
            smem,
            smem,
            smem,
            smem,
            pl.BlockSpec((2, BEAMS_HERE, WINDOWS_STEP * RAW_WINDOW), lambda i: (0, 0, i)),
        ],
        out_specs=[
            pl.BlockSpec((WINDOWS_STEP, 32, LANES), lambda i: (i, 0, 0)),
            pl.BlockSpec((TX, BEAM, 16, LANES), lambda i: (0, 0, 0, 0)),
        ],
        out_shape=[
            jax.ShapeDtypeStruct((WINDOWS, 32, LANES), BF16),
            jax.ShapeDtypeStruct((TX, BEAM, 16, LANES), BF16),
        ],
        scratch_shapes=[
            pltpu.VMEM((5 * LANES, 2 * LANES), BF16),
            pltpu.VMEM((2, BEAMS_HERE, LANES), BF16),
            pltpu.VMEM(((WINDOWS + 8) * 32, LANES), F32),
        ],
        name="front",
    )(tx_owner, delay_start, surv_taps.astype(F32), ref_taps.astype(F32), x)


def main_kernel(
    doppler,
    surv,
    ref_in,
    roots,
    out,
    gathered,
    reduced,
    refs,
    rows,
    corr_re,
    corr_im,
    table,
    outbox,
    inbox,
    send_a,
    recv_a,
    send_b,
    recv_b,
    send_c,
    recv_c,
):
    my_beam = lax.axis_index("beam")
    my_seg = lax.axis_index("seg")

    barrier = pltpu.get_barrier_semaphore()
    for o in range(1, BEAM):
        peer = lax.rem(my_beam + o, BEAM)
        pl.semaphore_signal(barrier, inc=1, device_id={"beam": peer}, device_id_type=MESH)
    for o in range(1, SEG):
        peer = lax.rem(my_seg + o, SEG)
        pl.semaphore_signal(barrier, inc=1, device_id={"seg": peer}, device_id_type=MESH)
    pl.semaphore_wait(barrier, BEAM - 1 + SEG - 1)

    def scatter(o):
        peer = lax.rem(my_beam + o, BEAM)
        return pltpu.make_async_remote_copy(
            src_ref=ref_in.at[:, peer],
            dst_ref=gathered.at[o],
            send_sem=send_a.at[o],
            recv_sem=recv_a.at[o],
            device_id={"beam": peer},
            device_id_type=MESH,
        )

    def spread(o):
        peer = lax.rem(my_beam + o, BEAM)
        return pltpu.make_async_remote_copy(
            src_ref=reduced,
            dst_ref=refs.at[:, my_beam],
            send_sem=send_b.at[o],
            recv_sem=recv_b.at[o],
            device_id={"beam": peer},
            device_id_type=MESH,
        )

    for o in range(1, BEAM):
        scatter(o).start()
    total = ref_in[:, my_beam].astype(F32)
    for o in range(1, BEAM):
        scatter(o).wait_recv()
        total = total + gathered[o].astype(F32)
    reduced[...] = total.astype(BF16)
    for o in range(1, BEAM):
        spread(o).start()
    refs[:, my_beam] = reduced[...]
    for o in range(1, BEAM):
        spread(o).wait_recv()
    for o in range(1, BEAM):
        scatter(o).wait_send()
        spread(o).wait_send()

    for k in range(TX):
        for part in range(2):
            flat = refs[k, part * 8 : (part + 1) * 8].reshape(WINDOWS, LANES)
            rows[2 * k + part, :WINDOWS] = flat.astype(F32)
            rows[2 * k + part, WINDOWS:] = jnp.zeros((8, LANES), F32)

    lane = lax.broadcasted_iota(jnp.int32, (16, LANES), 1)
    sub = lax.broadcasted_iota(jnp.int32, (16, LANES), 0)
    low = lax.broadcasted_iota(jnp.int32, (32, LANES), 1) < BLOCK_LEN
    nil = jnp.zeros((32, LANES), BF16)

    def share(k, o):
        peer = lax.rem(my_seg + o, SEG)
        return pltpu.make_async_remote_copy(
            src_ref=outbox.at[k, peer],
            dst_ref=inbox.at[k, o],
            send_sem=send_c.at[k, o],
            recv_sem=recv_c.at[k, o],
            device_id={"seg": peer},
            device_id_type=MESH,
        )

    def staggered(kp, i):
        row = jnp.broadcast_to(rows[kp, pl.ds(i, 1), :], (8, LANES))
        top = pltpu.roll(row, 1, axis=1, stride=1, stride_axis=0)
        bottom = pltpu.roll(top, 8, axis=1)
        return jnp.concatenate([top, bottom], axis=0).astype(BF16)

    def toeplitz(below, above):
        tiles = []
        for c in range(8):
            mixed = jnp.where((lane < sub + 1) | (lane >= LANES - 16 * c), below, above)
            tiles.append(pltpu.roll(mixed, 16 * c, axis=1) if c else mixed)
        return jnp.concatenate(tiles, axis=0)

    def transmitter(k, _):
        def pair(step, _):
            stag = [
                [staggered(2 * k + part, WINDOWS - 4 * step - r) for r in range(5)]
                for part in range(2)
            ]
            for sub_q in range(2):
                quad = 2 * step + sub_q
                halves = []
                for a in range(2):
                    r = 2 * sub_q + a
                    halves.append(
                        jnp.concatenate(
                            [toeplitz(stag[part][r + 1], stag[part][r]) for part in range(2)],
                            axis=1,
                        )
                    )
                right = jnp.concatenate(halves, axis=0)
                s0 = surv[2 * quad]
                s1 = surv[2 * quad + 1]
                left = jnp.concatenate(
                    [
                        jnp.concatenate([jnp.where(low, s0, nil), nil], axis=1),
                        jnp.concatenate([jnp.where(low, nil, s0), nil], axis=1),
                        jnp.concatenate([nil, jnp.where(low, s1, nil)], axis=1),
                        jnp.concatenate([nil, jnp.where(low, nil, s1)], axis=1),
                    ],
                    axis=0,
                )
                prod = jnp.dot(left, right, preferred_element_type=F32)
                for l in range(4):
                    re = prod[32 * l : 32 * l + 16]
                    im = prod[32 * l + 16 : 32 * l + 32]
                    at = 4 * quad + l
                    corr_re[pl.ds(at, BEAMS_HERE, stride=BLOCKS), :] = re[:, :LANES] + im[:, LANES:]
                    corr_im[pl.ds(at, BEAMS_HERE, stride=BLOCKS), :] = im[:, :LANES] - re[:, LANES:]
            return 0

        lax.fori_loop(0, WINDOWS // 4, pair, 0)

        for c in range(4):
            piece = roots[pl.ds(4 * doppler[k] + c, DOPPLER, stride=4), :].astype(BF16)
            table[:DOPPLER, c * LANES : (c + 1) * LANES] = piece
            if c < 2:
                table[DOPPLER:, BLOCKS + c * LANES : BLOCKS + (c + 1) * LANES] = piece
            else:
                table[DOPPLER:, (c - 2) * LANES : (c - 1) * LANES] = -piece

        def beams(bp, _):
            at = pl.multiple_of(bp * 2 * BLOCKS, 2 * BLOCKS)
            re = corr_re[pl.ds(at, 2 * BLOCKS), :].astype(BF16)
            im = corr_im[pl.ds(at, 2 * BLOCKS), :].astype(BF16)
            right = jnp.concatenate(
                [
                    jnp.concatenate([re[:BLOCKS], re[BLOCKS:]], axis=1),
                    jnp.concatenate([im[:BLOCKS], im[BLOCKS:]], axis=1),
                ],
                axis=0,
            )
            spec = jnp.dot(table[...], right, preferred_element_type=F32)
            sre, sim = spec[:DOPPLER], spec[DOPPLER:]
            power = (sre * sre + sim * sim) * (1.0 / (4 * BLOCKS * BLOCK_LEN))
            for b in range(2):
                turned = power[:, b * LANES : (b + 1) * LANES].T.astype(BF16)
                for g in range(SEG):
                    outbox[k, g, 2 * bp + b] = turned[16 * g : 16 * (g + 1)]
            return 0

        lax.fori_loop(0, BEAMS_HERE // 2, beams, 0)
        for o in range(1, SEG):
            share(k, o).start()
        return 0

    lax.fori_loop(0, TX, transmitter, 0)

    def collect(k, _):
        total = outbox[k, my_seg].astype(F32)
        for o in range(1, SEG):
            share(k, o).wait_recv()
            total = total + inbox[k, o].astype(F32)
        out[k] = total * (1.0 / SEG)
        for o in range(1, SEG):
            share(k, o).wait_send()
        return 0

    lax.fori_loop(0, TX, collect, 0)


def root_table():
    ells = np.arange(BLOCKS)[None, :]
    freqs = np.arange(2 * DOPPLER)[:, None] - BLOCKS // 2
    angle = 2.0 * np.pi / BLOCKS * ((ells * freqs) % BLOCKS)
    both = np.concatenate([np.cos(angle), np.sin(angle)], axis=1)
    return jnp.asarray(both.reshape(8 * DOPPLER, LANES), F32)


def ambiguity(doppler_start, surv, ref):
    vmem = pl.BlockSpec(memory_space=pltpu.VMEM)
    return pl.pallas_call(
        main_kernel,
        in_specs=[pl.BlockSpec(memory_space=pltpu.SMEM), vmem, vmem, vmem],
        out_specs=vmem,
        out_shape=jax.ShapeDtypeStruct((TX, BEAMS_HERE, DELAYS // SEG, DOPPLER), F32),
        scratch_shapes=[
            pltpu.VMEM((BEAM, TX, 16, LANES), BF16),
            pltpu.VMEM((TX, 16, LANES), BF16),
            pltpu.VMEM((TX, BEAM, 16, LANES), BF16),
            pltpu.VMEM((2 * TX, WINDOWS + 8, LANES), F32),
            pltpu.VMEM((BEAMS_HERE * BLOCKS, LANES), F32),
            pltpu.VMEM((BEAMS_HERE * BLOCKS, LANES), F32),
            pltpu.VMEM((2 * DOPPLER, 2 * BLOCKS), BF16),
            pltpu.VMEM((TX, SEG, BEAMS_HERE, 16, LANES), BF16),
            pltpu.VMEM((TX, SEG, BEAMS_HERE, 16, LANES), BF16),
            pltpu.SemaphoreType.DMA((BEAM,)),
            pltpu.SemaphoreType.DMA((BEAM,)),
            pltpu.SemaphoreType.DMA((BEAM,)),
            pltpu.SemaphoreType.DMA((BEAM,)),
            pltpu.SemaphoreType.DMA((TX, SEG)),
            pltpu.SemaphoreType.DMA((TX, SEG)),
        ],
        compiler_params=pltpu.CompilerParams(collective_id=0, has_side_effects=True),
        name="ambiguity",
    )(doppler_start, surv, ref, root_table())


def shards(voltages, surv_taps, ref_taps, tx_owner, delay_start, doppler_start):
    surv, ref = front(voltages, surv_taps, ref_taps, tx_owner, delay_start)
    return ambiguity(doppler_start, surv, ref)


def solution(mesh):
    return jax.shard_map(
        shards,
        mesh=mesh,
        in_specs=(P(None, "beam", "seg", None), P(), P(), P(), P(), P()),
        out_specs=P(None, "beam", "seg", None),
        check_vma=False,
    )
```

time: 678 us -> 119 us (0.18); the launches traced: 668 us -> 119 us
  waiting for transfers between devices: 260 us -> 0 us
  local copies, waits for them, and re-layouts: 242 us -> 1.87 us
  Pallas kernels: 0 us -> 115 us
  matrix products: 96.6 us -> 0 us
  other arithmetic: 39.1 us -> 2.36 us
  between operations: 29.2 us -> 0.01 us
    reduce_scatter x4 -> x0, waiting for transfers between devices: 168 us -> none  [shards(): summed = lax.psum_scatter(power, 'seg', scatter_dimension=1, tiled=True)]
    another operation x16 -> x0, local copies, waits for them, and re-layouts: 116 us -> none  [the longest x8 82.7 us: one_segment(): jnp.tile(window, (1, 1, BLOCK_LEN + 1))[..., :BLOCK_LEN * (span + 1)]]
    pallas_call x0 -> x2, Pallas kernels: none -> 115 us  [the longest x1 106 us: ambiguity(): pl.pallas_call(main_kernel, in_specs=[pl.BlockSpec(memory_space=pltpu.SME...]
    dot_general x37 -> x0, matrix products: 96.6 us -> none  [the longest x32 89.7 us: partial_einsum(): return jnp.einsum(form, left, right, preferred_element_type=jnp.float32)]
    psum x1 -> x0, waiting for transfers between devices: 91.9 us -> none  [from_root(): return lax.psum(kept, axis)]
    unnamed x59 -> x1, local copies, waits for them, and re-layouts: 58.7 us -> 1.87 us
    slice x28 -> x0, local copies, waits for them, and re-layouts: 39.9 us -> none  [the longest x8 18.3 us: one_segment(): jnp.tile(window, (1, 1, BLOCK_LEN + 1))[..., :BLOCK_LEN * (span + 1)]]
    convert_element_type x10 -> x2, other arithmetic: 17 us -> 2.36 us  [the longest x1 1.19 us: front(): ref_taps.astype(F32)]
  transfers between devices with their start and end apart: 5 -> 0, of which waited for: 4 -> 0; matrix products, arithmetic and copies ran while one was open for 27% -> 0% of each run, Pallas kernels for 0% -> 0%
where the time goes in v1:
time: 119 us
  Pallas kernels  115 us (97%)
  other arithmetic  2.36 us (2%)
  local copies, waits for them, and re-layouts  1.87 us (2%)
    pallas_call x1, Pallas kernels, ambiguity(): pl.pallas_call(main_kernel, in_specs=[pl.BlockSpec(memory_space=pltpu.SME...  106 us
    pallas_call x1, Pallas kernels, front(): pl.pallas_call(front_kernel, grid=(STEPS,), in_specs=[smem, smem, smem, s...  8.88 us

profile of v1, /device:TPU:0, one launch (start us, length us, event | category | flops | bytes accessed | tf_op | source)
XLA Modules:
  0.0 118.8 jit_solution(11276275583797991244)
XLA Ops:
  0.0 1.2 convert_element_type.6.surv_taps
  1.2 1.2 %convert_element_type.7.ref_taps = f32[32]{0:T(128)} convert(bf16[32]{0:T(256)(128)(2,1)} %param.9) | non-fusion elementwise | flops 32 | bytes 192 | tf_op jit(solution)/shard_map/convert_element_type | solution.py:137
  2.4 8.9 %front.1 = (bf16[128,32,128]{2,1,0:T(8,128)(2,1)}, bf16[4,16,16,128]{3,2,1,0:T(8,128)(2,1)}) custom-call(s32[4]{0:T(128)} %owner.1, s32[4]{0:T(128)} %delay.1, f32[32]{0:T(128)} %convert_element_type.6.surv_taps, f32[32]{0:T(128)} %convert_element_type.7.ref_taps, bf16[2,16,65536]{2,1,0:T(8,128)(2,1)} %bitcast.1), custom_call_target="tpu_custom_call" | custom-call | tf_op jit(solution)/shard_map/front/pallas_call | solution.py:113
  11.2 105.7 %ambiguity.1 = f32[4,16,16,128]{3,2,1,0:T(8,128)} custom-call(s32[4]{0:T(128)} %doppler.1, bf16[128,32,128]{2,1,0:T(8,128)(2,1)} %get-tuple-element.7.surv, bf16[4,16,16,128]{3,2,1,0:T(8,128)(2,1)} %get-tuple-element.8.ref_in, f32[1024,128]{1,0:T(8,128)} %constant.2.clone.roots), custom_call_target="tpu_custom_call" | custom-call | tf_op jit(solution)/shard_map/ambiguity/pallas_call | solution.py:345
  116.9 1.9 %copy.9 = f32[4,16,16,128]{3,2,1,0:T(8,128)} copy(f32[4,16,16,128]{3,2,1,0:T(8,128)} %ambiguity.1) | data formatting | bytes 1048576

commit v2 on v1

--- a/solution.py
+++ b/solution.py
@@ -18,11 +18,13 @@
 LANES = 128
 BEAMS_HERE = 16
 WINDOWS = 128
-WINDOWS_STEP = 16
+WINDOWS_STEP = 32
 STEPS = WINDOWS // WINDOWS_STEP
 RAW_WINDOW = DECIM * LANES
+REGION = (WINDOWS + 8) * 8
 BEAM = 16
 SEG = 8
+QUADS = 64
 F32 = jnp.float32
 BF16 = jnp.bfloat16
 MESH = pl.DeviceIdType.MESH
@@ -36,7 +38,7 @@
     offset = DECIM * cols - rows
     total = jnp.zeros((LANES, LANES), F32)
     for tap in range(TAPS):
-        total = jnp.where(offset == tap, taps[tap], total)
+        total = jnp.where(offset == tap, taps[tap].astype(F32), total)
     return total
 
 
@@ -62,9 +64,10 @@
             band[part * LANES : (part + 1) * LANES, :LANES] = ahead.astype(BF16)
             band[part * LANES : (part + 1) * LANES, LANES:] = behind.astype(BF16)
         halo[...] = jnp.zeros_like(halo)
-        picked[WINDOWS * 32 :, :] = jnp.zeros((8 * 32, LANES), F32)
-
-    for half in range(2):
+        for r in range(4):
+            picked[r * REGION + WINDOWS * 8 : (r + 1) * REGION, :] = jnp.zeros((64, LANES), F32)
+
+    for half in range(WINDOWS_STEP // 8):
         pieces = []
         for w in range(8):
             q = half * 8 + w
@@ -81,8 +84,9 @@
             q = half * 8 + w
             rows = out[w * 32 : (w + 1) * 32]
             surv[q] = rows[:, :LANES].astype(BF16)
-            at = pl.multiple_of((WINDOWS - 1 - WINDOWS_STEP * step - q) * 32, 32)
-            picked[pl.ds(at, 32), :] = rows[:, LANES:]
+            at = pl.multiple_of((WINDOWS - 1 - WINDOWS_STEP * step - q) * 8, 8)
+            for r in range(4):
+                picked[pl.ds(at + r * REGION, 8), :] = rows[8 * r : 8 * r + 8, LANES:]
     for part in range(2):
         halo[part] = x[part, :, WINDOWS_STEP * RAW_WINDOW - LANES :]
 
@@ -95,9 +99,9 @@
             rest = lax.rem(delay[k], LANES)
             turn = lax.rem(LANES - rest, LANES)
             for part in range(2):
-                start = whole * 32 + part * BEAMS_HERE + local
-                first = picked[pl.ds(start, WINDOWS, stride=32), :]
-                second = picked[pl.ds(start + 32, WINDOWS, stride=32), :]
+                start = (2 * part + lax.div(local, 8)) * REGION + whole * 8 + lax.rem(local, 8)
+                first = picked[pl.ds(start, WINDOWS, stride=8), :]
+                second = picked[pl.ds(start + 8, WINDOWS, stride=8), :]
                 moved = jnp.where(
                     lane < LANES - rest,
                     pltpu.roll(first, turn, axis=1),
@@ -131,10 +135,10 @@
         scratch_shapes=[
             pltpu.VMEM((5 * LANES, 2 * LANES), BF16),
             pltpu.VMEM((2, BEAMS_HERE, LANES), BF16),
-            pltpu.VMEM(((WINDOWS + 8) * 32, LANES), F32),
+            pltpu.VMEM((4 * REGION, LANES), F32),
         ],
         name="front",
-    )(tx_owner, delay_start, surv_taps.astype(F32), ref_taps.astype(F32), x)
+    )(tx_owner, delay_start, surv_taps, ref_taps, x)
 
 
 def main_kernel(
@@ -247,11 +251,11 @@
     def transmitter(k, _):
         def pair(step, _):
             stag = [
-                [staggered(2 * k + part, WINDOWS - 4 * step - r) for r in range(5)]
+                [staggered(2 * k + part, WINDOWS - 2 * QUADS * step - r) for r in range(2 * QUADS + 1)]
                 for part in range(2)
             ]
-            for sub_q in range(2):
-                quad = 2 * step + sub_q
+            for sub_q in range(QUADS):
+                quad = QUADS * step + sub_q
                 halves = []
                 for a in range(2):
                     r = 2 * sub_q + a
@@ -277,12 +281,15 @@
                 for l in range(4):
                     re = prod[32 * l : 32 * l + 16]
                     im = prod[32 * l + 16 : 32 * l + 32]
-                    at = 4 * quad + l
-                    corr_re[pl.ds(at, BEAMS_HERE, stride=BLOCKS), :] = re[:, :LANES] + im[:, LANES:]
-                    corr_im[pl.ds(at, BEAMS_HERE, stride=BLOCKS), :] = im[:, :LANES] - re[:, LANES:]
+                    cre = re[:, :LANES] + im[:, LANES:]
+                    cim = im[:, :LANES] - re[:, LANES:]
+                    for half in range(2):
+                        at = pl.multiple_of((4 * quad + l) * 8, 8) + half * 8 * BLOCKS
+                        corr_re[pl.ds(at, 8), :] = cre[8 * half : 8 * half + 8]
+                        corr_im[pl.ds(at, 8), :] = cim[8 * half : 8 * half + 8]
             return 0
 
-        lax.fori_loop(0, WINDOWS // 4, pair, 0)
+        lax.fori_loop(0, WINDOWS // (2 * QUADS), pair, 0)
 
         for c in range(4):
             piece = roots[pl.ds(4 * doppler[k] + c, DOPPLER, stride=4), :].astype(BF16)
@@ -292,27 +299,29 @@
             else:
                 table[DOPPLER:, (c - 2) * LANES : (c - 1) * LANES] = -piece
 
-        def beams(bp, _):
-            at = pl.multiple_of(bp * 2 * BLOCKS, 2 * BLOCKS)
-            re = corr_re[pl.ds(at, 2 * BLOCKS), :].astype(BF16)
-            im = corr_im[pl.ds(at, 2 * BLOCKS), :].astype(BF16)
-            right = jnp.concatenate(
-                [
-                    jnp.concatenate([re[:BLOCKS], re[BLOCKS:]], axis=1),
-                    jnp.concatenate([im[:BLOCKS], im[BLOCKS:]], axis=1),
-                ],
-                axis=0,
-            )
-            spec = jnp.dot(table[...], right, preferred_element_type=F32)
-            sre, sim = spec[:DOPPLER], spec[DOPPLER:]
-            power = (sre * sre + sim * sim) * (1.0 / (4 * BLOCKS * BLOCK_LEN))
-            for b in range(2):
-                turned = power[:, b * LANES : (b + 1) * LANES].T.astype(BF16)
-                for g in range(SEG):
-                    outbox[k, g, 2 * bp + b] = turned[16 * g : 16 * (g + 1)]
+        def beams(half, _):
+            def column(ref, b):
+                at = half * 8 * BLOCKS + b
+                return ref[pl.ds(at, BLOCKS, stride=8), :].astype(BF16)
+
+            for bp in range(4):
+                right = jnp.concatenate(
+                    [
+                        jnp.concatenate([column(ref, 2 * bp), column(ref, 2 * bp + 1)], axis=1)
+                        for ref in (corr_re, corr_im)
+                    ],
+                    axis=0,
+                )
+                spec = jnp.dot(table[...], right, preferred_element_type=F32)
+                sre, sim = spec[:DOPPLER], spec[DOPPLER:]
+                power = (sre * sre + sim * sim) * (1.0 / (4 * BLOCKS * BLOCK_LEN))
+                for b in range(2):
+                    turned = power[:, b * LANES : (b + 1) * LANES].T.astype(BF16)
+                    for g in range(SEG):
+                        outbox[k, g, 8 * half + 2 * bp + b] = turned[16 * g : 16 * (g + 1)]
             return 0
 
-        lax.fori_loop(0, BEAMS_HERE // 2, beams, 0)
+        lax.fori_loop(0, 2, beams, 0)
         for o in range(1, SEG):
             share(k, o).start()
         return 0

time: 119 us -> 58.7 us (0.49)
  Pallas kernels: 115 us -> 56.3 us
  other arithmetic: 2.36 us -> 0 us
    pallas_call x1, Pallas kernels: 106 us -> 50.2 us  [ambiguity(): pl.pallas_call(main_kernel, in_specs=[pl.BlockSpec(memory_space=pltpu.SME...]
    pallas_call x1, Pallas kernels: 8.88 us -> 6.06 us  [front(): pl.pallas_call(front_kernel, grid=(STEPS,), in_specs=[smem, smem, smem, s...]
    convert_element_type x2 -> x0, other arithmetic: 2.36 us -> none  [the longest x1 1.19 us: front(): ref_taps.astype(F32)]
where the time goes in v2:
time: 58.7 us; the launch traced here: 58.2 us
  Pallas kernels  56.3 us (96%)
  local copies, waits for them, and re-layouts  1.87 us (3%)
    pallas_call x1, Pallas kernels, ambiguity(): pl.pallas_call(main_kernel, in_specs=[pl.BlockSpec(memory_space=pltpu.SME...  50.2 us
    pallas_call x1, Pallas kernels, front(): pl.pallas_call(front_kernel, grid=(STEPS,), in_specs=[smem, smem, smem, s...  6.06 us
    unnamed x1, local copies, waits for them, and re-layouts  1.87 us

profile of v2, /device:TPU:0, one launch (start us, length us, event | category | flops | bytes accessed | tf_op | source)
XLA Modules:
  0.0 58.2 jit_solution(8357558306612614140)
XLA Ops:
  0.0 6.1 %front.1 = (bf16[128,32,128]{2,1,0:T(8,128)(2,1)}, bf16[4,16,16,128]{3,2,1,0:T(8,128)(2,1)}) custom-call(s32[4]{0:T(128)} %owner.1, s32[4]{0:T(128)} %delay.1, bf16[32]{0:T(256)(128)(2,1)} %surv_taps.1, bf16[32]{0:T(256)(128)(2,1)} %ref_taps.1, bf16[2,16,65536]{2,1,0:T(8,128)(2,1)} %bitcast.1), custom_call_target="tpu_custom_call" | custom-call | tf_op jit(solution)/shard_map/front/pallas_call | solution.py:117
  6.1 50.2 %ambiguity.1 = f32[4,16,16,128]{3,2,1,0:T(8,128)} custom-call(s32[4]{0:T(128)} %doppler.1, bf16[128,32,128]{2,1,0:T(8,128)(2,1)} %get-tuple-element.7.surv, bf16[4,16,16,128]{3,2,1,0:T(8,128)(2,1)} %get-tuple-element.8.ref_in, f32[1024,128]{1,0:T(8,128)} %constant.2.clone.roots), custom_call_target="tpu_custom_call" | custom-call | tf_op jit(solution)/shard_map/ambiguity/pallas_call | solution.py:354
  56.3 1.9 %copy.9 = f32[4,16,16,128]{3,2,1,0:T(8,128)} copy(f32[4,16,16,128]{3,2,1,0:T(8,128)} %ambiguity.1) | data formatting | bytes 1048576

commit v3 on v2

v3 whole, which is shorter than its diff:
```python
import functools

import jax
import jax.numpy as jnp
import numpy as np
from jax import lax
from jax.experimental import pallas as pl
from jax.experimental.pallas import tpu as pltpu
from jax.sharding import PartitionSpec as P

TX = 4
DECIM = 4
TAPS = 32
BLOCK_LEN = 64
BLOCKS = 256
DELAYS = 128
DOPPLER = 128
LANES = 128
BEAMS_HERE = 16
WINDOWS = 128
WINDOWS_STEP = 32
CHUNK = WINDOWS_STEP * 512
STEPS = WINDOWS // WINDOWS_STEP
RAW_WINDOW = DECIM * LANES
REGION = (WINDOWS + 8) * 8
BEAM = 16
SEG = 8
QUADS = 64
F32 = jnp.float32
BF16 = jnp.bfloat16
MESH = pl.DeviceIdType.MESH


def band_base(taps, backwards):
    rows = lax.broadcasted_iota(jnp.int32, (LANES, LANES), 0)
    cols = lax.broadcasted_iota(jnp.int32, (LANES, LANES), 1)
    if backwards:
        cols = LANES - 1 - cols
    offset = DECIM * cols - rows
    total = jnp.zeros((LANES, LANES), F32)
    for tap in range(TAPS):
        total = jnp.where(offset == tap, taps[tap].astype(F32), total)
    return total


def main_kernel(
    owner,
    delay,
    doppler,
    surv_taps,
    ref_taps,
    x_hbm,
    roots_hbm,
    out,
    x,
    roots,
    band,
    surv,
    picked,
    ref_in,
    gathered,
    reduced,
    refs,
    rows,
    corr_re,
    corr_im,
    table,
    outbox,
    inbox,
    sem_x,
    sem_roots,
    send_a,
    recv_a,
    send_b,
    recv_b,
    send_c,
    recv_c,
):
    my_beam = lax.axis_index("beam")
    my_seg = lax.axis_index("seg")

    def fetch(c):
        at = pl.multiple_of(c * CHUNK, LANES)
        return pltpu.make_async_copy(
            x_hbm.at[:, :, pl.ds(at, CHUNK)],
            x.at[:, :, pl.ds(at + LANES, CHUNK)],
            sem_x.at[c],
        )

    for c in range(STEPS):
        fetch(c).start()
    fetch_roots = pltpu.make_async_copy(roots_hbm, roots, sem_roots)
    fetch_roots.start()

    barrier = pltpu.get_barrier_semaphore()
    for o in range(1, BEAM):
        peer = lax.rem(my_beam + o, BEAM)
        pl.semaphore_signal(barrier, inc=1, device_id={"beam": peer}, device_id_type=MESH)
    for o in range(1, SEG):
        peer = lax.rem(my_seg + o, SEG)
        pl.semaphore_signal(barrier, inc=1, device_id={"seg": peer}, device_id_type=MESH)

    wide = lax.broadcasted_iota(jnp.int32, (LANES, LANES), 1)
    forward = band_base(surv_taps, False)
    backward = band_base(ref_taps, True)
    for part in range(5):
        shift = 32 * (part - 1)
        ahead = pltpu.roll(forward, shift % LANES, axis=1)
        behind = pltpu.roll(backward, -shift % LANES, axis=1)
        if part == 0:
            ahead = jnp.where(wide < 8, ahead, 0.0)
            behind = jnp.where(wide >= LANES - 8, behind, 0.0)
        else:
            ahead = jnp.where(wide >= shift, ahead, 0.0)
            behind = jnp.where(wide < LANES - shift, behind, 0.0)
        band[part * LANES : (part + 1) * LANES, :LANES] = ahead.astype(BF16)
        band[part * LANES : (part + 1) * LANES, LANES:] = behind.astype(BF16)
    x[:, :, :LANES] = jnp.zeros((2, BEAMS_HERE, LANES), BF16)
    for r in range(4):
        picked[r * REGION + WINDOWS * 8 : (r + 1) * REGION, :] = jnp.zeros((64, LANES), F32)

    def decimate(step, _):
        fetch(step).wait()
        for group in range(WINDOWS_STEP // 8):
            pieces = []
            for w in range(8):
                q = step * WINDOWS_STEP + group * 8 + w
                at = pl.multiple_of(q * RAW_WINDOW, LANES)
                for part in range(2):
                    pieces.append(x[part, :, pl.ds(at, RAW_WINDOW + LANES)])
            left = jnp.concatenate(pieces, axis=0)
            both = jnp.dot(left, band[...], preferred_element_type=F32)
            for w in range(8):
                q = step * WINDOWS_STEP + group * 8 + w
                part_rows = both[w * 32 : (w + 1) * 32]
                surv[q] = part_rows[:, :LANES].astype(BF16)
                at = pl.multiple_of((WINDOWS - 1 - q) * 8, 8)
                for r in range(4):
                    picked[pl.ds(at + r * REGION, 8), :] = part_rows[8 * r : 8 * r + 8, LANES:]
        return 0

    lax.fori_loop(0, STEPS, decimate, 0)

    def pick(k):
        mine = lax.div(owner[k], BEAMS_HERE) == my_beam
        local = lax.rem(owner[k], BEAMS_HERE)
        whole = lax.div(delay[k], LANES)
        rest = lax.rem(delay[k], LANES)
        turn = lax.rem(LANES - rest, LANES)
        for part in range(2):
            start = (2 * part + lax.div(local, 8)) * REGION + whole * 8 + lax.rem(local, 8)
            first = picked[pl.ds(start, WINDOWS, stride=8), :]
            second = picked[pl.ds(start + 8, WINDOWS, stride=8), :]
            moved = jnp.where(
                wide < LANES - rest,
                pltpu.roll(first, turn, axis=1),
                pltpu.roll(second, turn, axis=1),
            )
            moved = jnp.where(mine, moved, 0.0).astype(BF16)
            ref_in[k, part * 8 : (part + 1) * 8] = moved.reshape(8, 16, LANES)

    groups = ((0, 1), (1, 3))

    def scatter(g, o):
        base, count = groups[g]
        peer = lax.rem(my_beam + o, BEAM)
        return pltpu.make_async_remote_copy(
            src_ref=ref_in.at[pl.ds(base, count), peer],
            dst_ref=gathered.at[o, pl.ds(base, count)],
            send_sem=send_a.at[g, o],
            recv_sem=recv_a.at[g, o],
            device_id={"beam": peer},
            device_id_type=MESH,
        )

    def spread(g, o):
        base, count = groups[g]
        peer = lax.rem(my_beam + o, BEAM)
        return pltpu.make_async_remote_copy(
            src_ref=reduced.at[pl.ds(base, count)],
            dst_ref=refs.at[pl.ds(base, count), my_beam],
            send_sem=send_b.at[g, o],
            recv_sem=recv_b.at[g, o],
            device_id={"beam": peer},
            device_id_type=MESH,
        )

    def spread_sums(g):
        base, count = groups[g]
        total = ref_in[base : base + count, my_beam].astype(F32)
        for o in range(1, BEAM):
            scatter(g, o).wait_recv()
            total = total + gathered[o, base : base + count].astype(F32)
        reduced[base : base + count] = total.astype(BF16)
        for o in range(1, BEAM):
            spread(g, o).start()
        refs[base : base + count, my_beam] = reduced[base : base + count]

    def arrive(g):
        base, count = groups[g]
        for o in range(1, BEAM):
            spread(g, o).wait_recv()
        for k in range(base, base + count):
            for part in range(2):
                flat = refs[k, part * 8 : (part + 1) * 8].reshape(WINDOWS, LANES)
                rows[2 * k + part, :WINDOWS] = flat.astype(F32)
                rows[2 * k + part, WINDOWS:] = jnp.zeros((8, LANES), F32)

    pick(0)
    pl.semaphore_wait(barrier, BEAM - 1 + SEG - 1)
    for o in range(1, BEAM):
        scatter(0, o).start()
    for k in range(1, TX):
        pick(k)
    for o in range(1, BEAM):
        scatter(1, o).start()
    fetch_roots.wait()
    spread_sums(0)
    spread_sums(1)
    arrive(0)

    lane = lax.broadcasted_iota(jnp.int32, (16, LANES), 1)
    sub = lax.broadcasted_iota(jnp.int32, (16, LANES), 0)
    low = lax.broadcasted_iota(jnp.int32, (32, LANES), 1) < BLOCK_LEN
    nil = jnp.zeros((32, LANES), BF16)

    def share(k, half, o):
        peer = lax.rem(my_seg + o, SEG)
        at = pl.multiple_of(half * 8, 8)
        return pltpu.make_async_remote_copy(
            src_ref=outbox.at[k, peer, pl.ds(at, 8)],
            dst_ref=inbox.at[k, o, pl.ds(at, 8)],
            send_sem=send_c.at[k, half, o],
            recv_sem=recv_c.at[k, half, o],
            device_id={"seg": peer},
            device_id_type=MESH,
        )

    def staggered(kp, i):
        row = jnp.broadcast_to(rows[kp, pl.ds(i, 1), :], (8, LANES))
        top = pltpu.roll(row, 1, axis=1, stride=1, stride_axis=0)
        bottom = pltpu.roll(top, 8, axis=1)
        return jnp.concatenate([top, bottom], axis=0).astype(BF16)

    def toeplitz(below, above):
        tiles = []
        for c in range(8):
            mixed = jnp.where((lane < sub + 1) | (lane >= LANES - 16 * c), below, above)
            tiles.append(pltpu.roll(mixed, 16 * c, axis=1) if c else mixed)
        return jnp.concatenate(tiles, axis=0)

    def transmitter(k, _):
        def pair(step, _):
            stag = [
                [staggered(2 * k + part, WINDOWS - 2 * QUADS * step - r) for r in range(2 * QUADS + 1)]
                for part in range(2)
            ]
            for sub_q in range(QUADS):
                quad = QUADS * step + sub_q
                halves = []
                for a in range(2):
                    r = 2 * sub_q + a
                    halves.append(
                        jnp.concatenate(
                            [toeplitz(stag[part][r + 1], stag[part][r]) for part in range(2)],
                            axis=1,
                        )
                    )
                right = jnp.concatenate(halves, axis=0)
                s0 = surv[2 * quad]
                s1 = surv[2 * quad + 1]
                left = jnp.concatenate(
                    [
                        jnp.concatenate([jnp.where(low, s0, nil), nil], axis=1),
                        jnp.concatenate([jnp.where(low, nil, s0), nil], axis=1),
                        jnp.concatenate([nil, jnp.where(low, s1, nil)], axis=1),
                        jnp.concatenate([nil, jnp.where(low, nil, s1)], axis=1),
                    ],
                    axis=0,
                )
                prod = jnp.dot(left, right, preferred_element_type=F32)
                for l in range(4):
                    re = prod[32 * l : 32 * l + 16]
                    im = prod[32 * l + 16 : 32 * l + 32]
                    cre = re[:, :LANES] + im[:, LANES:]
                    cim = im[:, :LANES] - re[:, LANES:]
                    for half in range(2):
                        at = pl.multiple_of((4 * quad + l) * 8, 8) + half * 8 * BLOCKS
                        corr_re[pl.ds(at, 8), :] = cre[8 * half : 8 * half + 8]
                        corr_im[pl.ds(at, 8), :] = cim[8 * half : 8 * half + 8]
            return 0

        lax.fori_loop(0, WINDOWS // (2 * QUADS), pair, 0)

        for c in range(4):
            piece = roots[pl.ds(4 * doppler[k] + c, DOPPLER, stride=4), :].astype(BF16)
            table[:DOPPLER, c * LANES : (c + 1) * LANES] = piece
            if c < 2:
                table[DOPPLER:, BLOCKS + c * LANES : BLOCKS + (c + 1) * LANES] = piece
            else:
                table[DOPPLER:, (c - 2) * LANES : (c - 1) * LANES] = -piece

        def beams(half, _):
            def column(ref, b):
                at = half * 8 * BLOCKS + b
                return ref[pl.ds(at, BLOCKS, stride=8), :].astype(BF16)

            for bp in range(4):
                right = jnp.concatenate(
                    [
                        jnp.concatenate([column(ref, 2 * bp), column(ref, 2 * bp + 1)], axis=1)
                        for ref in (corr_re, corr_im)
                    ],
                    axis=0,
                )
                spec = jnp.dot(table[...], right, preferred_element_type=F32)
                sre, sim = spec[:DOPPLER], spec[DOPPLER:]
                power = (sre * sre + sim * sim) * (1.0 / (4 * BLOCKS * BLOCK_LEN))
                for b in range(2):
                    turned = power[:, b * LANES : (b + 1) * LANES].T.astype(BF16)
                    for g in range(SEG):
                        outbox[k, g, 8 * half + 2 * bp + b] = turned[16 * g : 16 * (g + 1)]
            for o in range(1, SEG):
                share(k, half, o).start()
            return 0

        lax.fori_loop(0, 2, beams, 0)

        @pl.when(k == 0)
        def _():
            arrive(1)

        return 0

    lax.fori_loop(0, TX, transmitter, 0)

    for g in range(2):
        for o in range(1, BEAM):
            scatter(g, o).wait_send()
            spread(g, o).wait_send()

    def collect(k, _):
        for half in range(2):
            beams_half = slice(8 * half, 8 * half + 8)
            total = outbox[k, my_seg, beams_half].astype(F32)
            for o in range(1, SEG):
                share(k, half, o).wait_recv()
                total = total + inbox[k, o, beams_half].astype(F32)
            out[k, beams_half] = total * (1.0 / SEG)
            for o in range(1, SEG):
                share(k, half, o).wait_send()
        return 0

    lax.fori_loop(0, TX, collect, 0)


def root_table():
    ells = np.arange(BLOCKS)[None, :]
    freqs = np.arange(2 * DOPPLER)[:, None] - BLOCKS // 2
    angle = 2.0 * np.pi / BLOCKS * ((ells * freqs) % BLOCKS)
    both = np.concatenate([np.cos(angle), np.sin(angle)], axis=1)
    return jnp.asarray(both.reshape(8 * DOPPLER, LANES), F32)


def shards(voltages, surv_taps, ref_taps, tx_owner, delay_start, doppler_start):
    smem = pl.BlockSpec(memory_space=pltpu.SMEM)
    hbm = pl.BlockSpec(memory_space=pl.ANY)
    dma = pltpu.SemaphoreType.DMA
    raw = DECIM * WINDOWS * LANES
    return pl.pallas_call(
        main_kernel,
        in_specs=[smem] * 5 + [hbm] * 2,
        out_specs=pl.BlockSpec(memory_space=pltpu.VMEM),
        out_shape=jax.ShapeDtypeStruct((TX, BEAMS_HERE, DELAYS // SEG, DOPPLER), F32),
        scratch_shapes=[
            pltpu.VMEM((2, BEAMS_HERE, raw + LANES), BF16),
            pltpu.VMEM((8 * DOPPLER, LANES), F32),
            pltpu.VMEM((5 * LANES, 2 * LANES), BF16),
            pltpu.VMEM((WINDOWS, 32, LANES), BF16),
            pltpu.VMEM((4 * REGION, LANES), F32),
            pltpu.VMEM((TX, BEAM, 16, LANES), BF16),
            pltpu.VMEM((BEAM, TX, 16, LANES), BF16),
            pltpu.VMEM((TX, 16, LANES), BF16),
            pltpu.VMEM((TX, BEAM, 16, LANES), BF16),
            pltpu.VMEM((2 * TX, WINDOWS + 8, LANES), F32),
            pltpu.VMEM((BEAMS_HERE * BLOCKS, LANES), F32),
            pltpu.VMEM((BEAMS_HERE * BLOCKS, LANES), F32),
            pltpu.VMEM((2 * DOPPLER, 2 * BLOCKS), BF16),
            pltpu.VMEM((TX, SEG, BEAMS_HERE, 16, LANES), BF16),
            pltpu.VMEM((TX, SEG, BEAMS_HERE, 16, LANES), BF16),
            dma((STEPS,)),
            dma,
            dma((2, BEAM)),
            dma((2, BEAM)),
            dma((2, BEAM)),
            dma((2, BEAM)),
            dma((TX, 2, SEG)),
            dma((TX, 2, SEG)),
        ],
        compiler_params=pltpu.CompilerParams(collective_id=0, has_side_effects=True),
        name="ambiguity",
    )(
        tx_owner,
        delay_start,
        doppler_start,
        surv_taps,
        ref_taps,
        voltages.reshape(2, BEAMS_HERE, raw),
        root_table(),
    )


def solution(mesh):
    return jax.shard_map(
        shards,
        mesh=mesh,
        in_specs=(P(None, "beam", "seg", None), P(), P(), P(), P(), P()),
        out_specs=P(None, "beam", "seg", None),
        check_vma=False,
    )
```

time: 58.7 us -> 51.1 us (0.87)
  Pallas kernels: 56.3 us -> 49.1 us
    pallas_call x2 -> x1, Pallas kernels: 56.3 us -> 49.1 us  [shards(): pl.pallas_call(main_kernel, in_specs=[smem] * 5 + [hbm] * 2, out_specs=pl...]
where the time goes in v3:
time: 51.1 us; the launch traced here: 51 us
  Pallas kernels  49.1 us (96%)
  local copies, waits for them, and re-layouts  1.87 us (4%)
    pallas_call x1, Pallas kernels, shards(): pl.pallas_call(main_kernel, in_specs=[smem] * 5 + [hbm] * 2, out_specs=pl...  49.1 us
    unnamed x1, local copies, waits for them, and re-layouts  1.87 us

profile of v3, /device:TPU:0, one launch (start us, length us, event | category | flops | bytes accessed | tf_op | source)
XLA Modules:
  0.0 51.0 jit_solution(10876479689129468797)
XLA Ops:
  0.0 49.1 %ambiguity.1 = f32[4,16,16,128]{3,2,1,0:T(8,128)} custom-call(s32[4]{0:T(128)} %owner.1, s32[4]{0:T(128)} %delay.1, s32[4]{0:T(128)} %doppler.1, bf16[32]{0:T(256)(128)(2,1)} %surv_taps.1, bf16[32]{0:T(256)(128)(2,1)} %ref_taps.1, bf16[2,16,65536]{2,1,0:T(8,128)(2,1)} %bitcast.1, f32[1024,128]{1,0:T(8,128)} %constant.2.clone.roots_hbm), custom_call_target="tpu_custom_call" | custom-call | tf_op jit(solution)/shard_map/ambiguity/pallas_call | solution.py:370
  49.1 1.9 %copy.9 = f32[4,16,16,128]{3,2,1,0:T(8,128)} copy(f32[4,16,16,128]{3,2,1,0:T(8,128)} %ambiguity.1) | data formatting | bytes 1048576

commit v4 on v3

--- a/solution.py
+++ b/solution.py
@@ -66,7 +66,12 @@
     corr_im,
     table,
     outbox,
-    inbox,
+    in_x,
+    in_z,
+    sum_x,
+    sum_z,
+    last_x,
+    last_z,
     sem_x,
     sem_roots,
     send_a,
@@ -75,6 +80,8 @@
     recv_b,
     send_c,
     recv_c,
+    send_d,
+    recv_d,
 ):
     my_beam = lax.axis_index("beam")
     my_seg = lax.axis_index("seg")
@@ -224,17 +231,71 @@
     low = lax.broadcasted_iota(jnp.int32, (32, LANES), 1) < BLOCK_LEN
     nil = jnp.zeros((32, LANES), BF16)
 
-    def share(k, half, o):
-        peer = lax.rem(my_seg + o, SEG)
-        at = pl.multiple_of(half * 8, 8)
+    my_z = lax.div(my_seg, 2)
+    my_x = lax.rem(my_seg, 2)
+    other = {"seg": 2 * my_z + 1 - my_x}
+
+    def ring(dz):
+        z = lax.rem(my_z + dz, 4)
+        return z, {"seg": 2 * z + my_x}
+
+    def remote(src, dst, send, recv, device):
         return pltpu.make_async_remote_copy(
-            src_ref=outbox.at[k, peer, pl.ds(at, 8)],
-            dst_ref=inbox.at[k, o, pl.ds(at, 8)],
-            send_sem=send_c.at[k, half, o],
-            recv_sem=recv_c.at[k, half, o],
-            device_id={"seg": peer},
+            src_ref=src,
+            dst_ref=dst,
+            send_sem=send,
+            recv_sem=recv,
+            device_id=device,
             device_id_type=MESH,
         )
+
+    def across(k):
+        return remote(
+            outbox.at[k, 0, :, 1 - my_x], in_x.at[k], send_c.at[k, 0], recv_c.at[k, 0], other
+        )
+
+    def around(k, dz):
+        z, device = ring(dz)
+        return remote(
+            outbox.at[k, 1, z], in_z.at[k, dz], send_c.at[k, dz], recv_c.at[k, dz], device
+        )
+
+    def across_last(k):
+        return remote(
+            sum_z.at[k, 1 - my_x], last_x.at[k], send_d.at[k, 0], recv_d.at[k, 0], other
+        )
+
+    def around_last(k, dz):
+        z, device = ring(dz)
+        return remote(
+            sum_x.at[k, z], last_z.at[k, dz], send_d.at[k, dz], recv_d.at[k, dz], device
+        )
+
+    def second(k):
+        across(k).wait_recv()
+        for z in range(4):
+            total = outbox[k, 0, z, my_x].astype(F32) + in_x[k, z].astype(F32)
+            sum_x[k, z] = total.astype(BF16)
+        for dz in range(1, 4):
+            around_last(k, dz).start()
+        for dz in range(1, 4):
+            around(k, dz).wait_recv()
+        for side in range(2):
+            total = outbox[k, 1, my_z, side].astype(F32)
+            for dz in range(1, 4):
+                total = total + in_z[k, dz, side].astype(F32)
+            sum_z[k, side] = total.astype(BF16)
+        across_last(k).start()
+
+    def first(k, half):
+        @pl.when(half == 0)
+        def _():
+            across(k).start()
+
+        @pl.when(half == 1)
+        def _():
+            for dz in range(1, 4):
+                around(k, dz).start()
 
     def staggered(kp, i):
         row = jnp.broadcast_to(rows[kp, pl.ds(i, 1), :], (8, LANES))
@@ -319,9 +380,8 @@
                 for b in range(2):
                     turned = power[:, b * LANES : (b + 1) * LANES].T.astype(BF16)
                     for g in range(SEG):
-                        outbox[k, g, 8 * half + 2 * bp + b] = turned[16 * g : 16 * (g + 1)]
-            for o in range(1, SEG):
-                share(k, half, o).start()
+                        outbox[k, half, g // 2, g % 2, 2 * bp + b] = turned[16 * g : 16 * (g + 1)]
+            first(k, half)
             return 0
 
         lax.fori_loop(0, 2, beams, 0)
@@ -329,6 +389,10 @@
         @pl.when(k == 0)
         def _():
             arrive(1)
+
+        @pl.when(k > 0)
+        def _():
+            second(k - 1)
 
         return 0
 
@@ -339,16 +403,22 @@
             scatter(g, o).wait_send()
             spread(g, o).wait_send()
 
+    second(TX - 1)
+
     def collect(k, _):
-        for half in range(2):
-            beams_half = slice(8 * half, 8 * half + 8)
-            total = outbox[k, my_seg, beams_half].astype(F32)
-            for o in range(1, SEG):
-                share(k, half, o).wait_recv()
-                total = total + inbox[k, o, beams_half].astype(F32)
-            out[k, beams_half] = total * (1.0 / SEG)
-            for o in range(1, SEG):
-                share(k, half, o).wait_send()
+        total = sum_x[k, my_z].astype(F32)
+        for dz in range(1, 4):
+            around_last(k, dz).wait_recv()
+            total = total + last_z[k, dz].astype(F32)
+        out[k, 0:8] = total * (1.0 / SEG)
+        across_last(k).wait_recv()
+        total = sum_z[k, my_x].astype(F32) + last_x[k].astype(F32)
+        out[k, 8:16] = total * (1.0 / SEG)
+        across(k).wait_send()
+        across_last(k).wait_send()
+        for dz in range(1, 4):
+            around(k, dz).wait_send()
+            around_last(k, dz).wait_send()
         return 0
 
     lax.fori_loop(0, TX, collect, 0)
@@ -386,16 +456,23 @@
             pltpu.VMEM((BEAMS_HERE * BLOCKS, LANES), F32),
             pltpu.VMEM((BEAMS_HERE * BLOCKS, LANES), F32),
             pltpu.VMEM((2 * DOPPLER, 2 * BLOCKS), BF16),
-            pltpu.VMEM((TX, SEG, BEAMS_HERE, 16, LANES), BF16),
-            pltpu.VMEM((TX, SEG, BEAMS_HERE, 16, LANES), BF16),
+            pltpu.VMEM((TX, 2, 4, 2, 8, 16, LANES), BF16),
+            pltpu.VMEM((TX, 4, 8, 16, LANES), BF16),
+            pltpu.VMEM((TX, 4, 2, 8, 16, LANES), BF16),
+            pltpu.VMEM((TX, 4, 8, 16, LANES), BF16),
+            pltpu.VMEM((TX, 2, 8, 16, LANES), BF16),
+            pltpu.VMEM((TX, 8, 16, LANES), BF16),
+            pltpu.VMEM((TX, 4, 8, 16, LANES), BF16),
             dma((STEPS,)),
             dma,
             dma((2, BEAM)),
             dma((2, BEAM)),
             dma((2, BEAM)),
             dma((2, BEAM)),
-            dma((TX, 2, SEG)),
-            dma((TX, 2, SEG)),
+            dma((TX, 4)),
+            dma((TX, 4)),
+            dma((TX, 4)),
+            dma((TX, 4)),
         ],
         compiler_params=pltpu.CompilerParams(collective_id=0, has_side_effects=True),
         name="ambiguity",

time: 51.1 us -> 49.1 us (0.961)
  Pallas kernels: 49.1 us -> 47.1 us
    pallas_call x1, Pallas kernels: 49.1 us -> 47.1 us  [shards(): pl.pallas_call(main_kernel, in_specs=[smem] * 5 + [hbm] * 2, out_specs=pl...]
where the time goes in v4:
time: 49.1 us; the launch traced here: 49 us
  Pallas kernels  47.1 us (96%)
  local copies, waits for them, and re-layouts  1.87 us (4%)
    pallas_call x1, Pallas kernels, shards(): pl.pallas_call(main_kernel, in_specs=[smem] * 5 + [hbm] * 2, out_specs=pl...  47.1 us
    unnamed x1, local copies, waits for them, and re-layouts  1.87 us

profile of v4, /device:TPU:0, one launch (start us, length us, event | category | flops | bytes accessed | tf_op | source)
XLA Modules:
  0.0 49.0 jit_solution(13582487980303810167)
XLA Ops:
  0.0 47.1 %ambiguity.1 = f32[4,16,16,128]{3,2,1,0:T(8,128)} custom-call(s32[4]{0:T(128)} %owner.1, s32[4]{0:T(128)} %delay.1, s32[4]{0:T(128)} %doppler.1, bf16[32]{0:T(256)(128)(2,1)} %surv_taps.1, bf16[32]{0:T(256)(128)(2,1)} %ref_taps.1, bf16[2,16,65536]{2,1,0:T(8,128)(2,1)} %bitcast.1, f32[1024,128]{1,0:T(8,128)} %constant.2.clone.roots_hbm), custom_call_target="tpu_custom_call" | custom-call | tf_op jit(solution)/shard_map/ambiguity/pallas_call | solution.py:440
  47.1 1.9 %copy.9 = f32[4,16,16,128]{3,2,1,0:T(8,128)} copy(f32[4,16,16,128]{3,2,1,0:T(8,128)} %ambiguity.1) | data formatting | bytes 1048576

commit v5 on v4

--- a/solution.py
+++ b/solution.py
@@ -62,6 +62,7 @@
     reduced,
     refs,
     rows,
+    leaning,
     corr_re,
     corr_im,
     table,
@@ -72,6 +73,7 @@
     sum_z,
     last_x,
     last_z,
+    inbox,
     sem_x,
     sem_roots,
     send_a,
@@ -82,6 +84,8 @@
     recv_c,
     send_d,
     recv_d,
+    send_e,
+    recv_e,
 ):
     my_beam = lax.axis_index("beam")
     my_seg = lax.axis_index("seg")
@@ -211,7 +215,18 @@
             for part in range(2):
                 flat = refs[k, part * 8 : (part + 1) * 8].reshape(WINDOWS, LANES)
                 rows[2 * k + part, :WINDOWS] = flat.astype(F32)
-                rows[2 * k + part, WINDOWS:] = jnp.zeros((8, LANES), F32)
+
+        def stagger(step, _):
+            for r in range(64):
+                kp = 2 * base + lax.div(step, 2)
+                i = lax.rem(step, 2) * 64 + r
+                row = jnp.broadcast_to(rows[kp, pl.ds(i, 1), :], (8, LANES))
+                top = pltpu.roll(row, 1, axis=1, stride=1, stride_axis=0)
+                bottom = pltpu.roll(row, 9, axis=1, stride=1, stride_axis=0)
+                leaning[kp, i] = jnp.concatenate([top, bottom], axis=0).astype(BF16)
+            return 0
+
+        lax.fori_loop(0, 4 * count, stagger, 0)
 
     pick(0)
     pl.semaphore_wait(barrier, BEAM - 1 + SEG - 1)
@@ -287,46 +302,66 @@
             sum_z[k, side] = total.astype(BF16)
         across_last(k).start()
 
+    def straight(half, o):
+        peer = lax.rem(my_seg + o, SEG)
+        return remote(
+            outbox.at[TX - 1, half, lax.div(peer, 2), lax.rem(peer, 2)],
+            inbox.at[half, o],
+            send_e.at[half, o],
+            recv_e.at[half, o],
+            {"seg": peer},
+        )
+
     def first(k, half):
-        @pl.when(half == 0)
+        @pl.when((half == 0) & (k < TX - 1))
         def _():
             across(k).start()
 
-        @pl.when(half == 1)
+        @pl.when((half == 1) & (k < TX - 1))
         def _():
             for dz in range(1, 4):
                 around(k, dz).start()
 
+        @pl.when(k == TX - 1)
+        def _():
+            for o in range(1, SEG):
+                straight(half, o).start()
+
+    for kp in range(2 * TX):
+        leaning[kp, WINDOWS] = jnp.zeros((16, LANES), BF16)
+
     def staggered(kp, i):
-        row = jnp.broadcast_to(rows[kp, pl.ds(i, 1), :], (8, LANES))
-        top = pltpu.roll(row, 1, axis=1, stride=1, stride_axis=0)
-        bottom = pltpu.roll(top, 8, axis=1)
-        return jnp.concatenate([top, bottom], axis=0).astype(BF16)
+        return leaning[kp, i]
+
+    def turns(u):
+        return [u] + [pltpu.roll(u, 16 * c, axis=1) for c in range(1, 4)]
 
     def toeplitz(below, above):
-        tiles = []
-        for c in range(8):
-            mixed = jnp.where((lane < sub + 1) | (lane >= LANES - 16 * c), below, above)
-            tiles.append(pltpu.roll(mixed, 16 * c, axis=1) if c else mixed)
-        return jnp.concatenate(tiles, axis=0)
+        even, odd = [], []
+        for c in range(4):
+            near = lane < sub + 1 + 16 * c
+            even.append(jnp.where(near, below[c], above[c]))
+            odd.append(jnp.where(near | (lane >= BLOCK_LEN), below[c], above[c]))
+        return jnp.concatenate(even + odd, axis=0)
 
     def transmitter(k, _):
         def pair(step, _):
-            stag = [
-                [staggered(2 * k + part, WINDOWS - 2 * QUADS * step - r) for r in range(2 * QUADS + 1)]
-                for part in range(2)
-            ]
+            def row_of(r):
+                return [turns(staggered(2 * k + part, WINDOWS - 2 * QUADS * step - r)) for part in range(2)]
+
+            above = row_of(0)
             for sub_q in range(QUADS):
                 quad = QUADS * step + sub_q
                 halves = []
                 for a in range(2):
                     r = 2 * sub_q + a
+                    below = row_of(r + 1)
                     halves.append(
                         jnp.concatenate(
-                            [toeplitz(stag[part][r + 1], stag[part][r]) for part in range(2)],
-                            axis=1,
+                            [toeplitz(below[part], above[part]) for part in range(2)], axis=1
                         )
                     )
+                    above = below
                 right = jnp.concatenate(halves, axis=0)
                 s0 = surv[2 * quad]
                 s1 = surv[2 * quad + 1]
@@ -346,7 +381,8 @@
                     cre = re[:, :LANES] + im[:, LANES:]
                     cim = im[:, :LANES] - re[:, LANES:]
                     for half in range(2):
-                        at = pl.multiple_of((4 * quad + l) * 8, 8) + half * 8 * BLOCKS
+                        at = pl.multiple_of((2 * quad + l // 2) * 8, 8) + (l % 2) * 4 * BLOCKS
+                        at = at + half * 8 * BLOCKS
                         corr_re[pl.ds(at, 8), :] = cre[8 * half : 8 * half + 8]
                         corr_im[pl.ds(at, 8), :] = cim[8 * half : 8 * half + 8]
             return 0
@@ -364,7 +400,9 @@
         def beams(half, _):
             def column(ref, b):
                 at = half * 8 * BLOCKS + b
-                return ref[pl.ds(at, BLOCKS, stride=8), :].astype(BF16)
+                even = ref[pl.ds(at, LANES, stride=8), :].astype(BF16)
+                odd = ref[pl.ds(at + 8 * LANES, LANES, stride=8), :].astype(BF16)
+                return jnp.concatenate([even, pltpu.roll(odd, BLOCK_LEN, axis=1)], axis=0)
 
             for bp in range(4):
                 right = jnp.concatenate(
@@ -403,8 +441,6 @@
             scatter(g, o).wait_send()
             spread(g, o).wait_send()
 
-    second(TX - 1)
-
     def collect(k, _):
         total = sum_x[k, my_z].astype(F32)
         for dz in range(1, 4):
@@ -421,11 +457,21 @@
             around_last(k, dz).wait_send()
         return 0
 
-    lax.fori_loop(0, TX, collect, 0)
+    lax.fori_loop(0, TX - 1, collect, 0)
+
+    for half in range(2):
+        total = outbox[TX - 1, half, my_z, my_x].astype(F32)
+        for o in range(1, SEG):
+            straight(half, o).wait_recv()
+            total = total + inbox[half, o].astype(F32)
+        out[TX - 1, 8 * half : 8 * half + 8] = total * (1.0 / SEG)
+    for half in range(2):
+        for o in range(1, SEG):
+            straight(half, o).wait_send()
 
 
 def root_table():
-    ells = np.arange(BLOCKS)[None, :]
+    ells = np.arange(BLOCKS).reshape(LANES, 2).T.reshape(1, BLOCKS)
     freqs = np.arange(2 * DOPPLER)[:, None] - BLOCKS // 2
     angle = 2.0 * np.pi / BLOCKS * ((ells * freqs) % BLOCKS)
     both = np.concatenate([np.cos(angle), np.sin(angle)], axis=1)
@@ -452,7 +498,8 @@
             pltpu.VMEM((BEAM, TX, 16, LANES), BF16),
             pltpu.VMEM((TX, 16, LANES), BF16),
             pltpu.VMEM((TX, BEAM, 16, LANES), BF16),
-            pltpu.VMEM((2 * TX, WINDOWS + 8, LANES), F32),
+            pltpu.VMEM((2 * TX, WINDOWS, LANES), F32),
+            pltpu.VMEM((2 * TX, WINDOWS + 1, 16, LANES), BF16),
             pltpu.VMEM((BEAMS_HERE * BLOCKS, LANES), F32),
             pltpu.VMEM((BEAMS_HERE * BLOCKS, LANES), F32),
             pltpu.VMEM((2 * DOPPLER, 2 * BLOCKS), BF16),
@@ -463,6 +510,7 @@
             pltpu.VMEM((TX, 2, 8, 16, LANES), BF16),
             pltpu.VMEM((TX, 8, 16, LANES), BF16),
             pltpu.VMEM((TX, 4, 8, 16, LANES), BF16),
+            pltpu.VMEM((2, SEG, 8, 16, LANES), BF16),
             dma((STEPS,)),
             dma,
             dma((2, BEAM)),
@@ -473,6 +521,8 @@
             dma((TX, 4)),
             dma((TX, 4)),
             dma((TX, 4)),
+            dma((2, SEG)),
+            dma((2, SEG)),
         ],
         compiler_params=pltpu.CompilerParams(collective_id=0, has_side_effects=True),
         name="ambiguity",

time: 49.1 us -> 47.5 us (0.967)
  Pallas kernels: 47.1 us -> 45.3 us
    pallas_call x1, Pallas kernels: 47.1 us -> 45.3 us  [shards(): pl.pallas_call(main_kernel, in_specs=[smem] * 5 + [hbm] * 2, out_specs=pl...]
where the time goes in v5:
time: 47.5 us; the launch traced here: 47.2 us
  Pallas kernels  45.3 us (95%)
  local copies, waits for them, and re-layouts  1.87 us (4%)
    pallas_call x1, Pallas kernels, shards(): pl.pallas_call(main_kernel, in_specs=[smem] * 5 + [hbm] * 2, out_specs=pl...  45.3 us
    unnamed x1, local copies, waits for them, and re-layouts  1.87 us

profile of v5, /device:TPU:0, one launch (start us, length us, event | category | flops | bytes accessed | tf_op | source)
XLA Modules:
  0.0 47.2 jit_solution(16140331665004144698)
XLA Ops:
  0.0 45.3 %ambiguity.1 = f32[4,16,16,128]{3,2,1,0:T(8,128)} custom-call(s32[4]{0:T(128)} %owner.1, s32[4]{0:T(128)} %delay.1, s32[4]{0:T(128)} %doppler.1, bf16[32]{0:T(256)(128)(2,1)} %surv_taps.1, bf16[32]{0:T(256)(128)(2,1)} %ref_taps.1, bf16[2,16,65536]{2,1,0:T(8,128)(2,1)} %bitcast.1, f32[1024,128]{1,0:T(8,128)} %constant.2.clone.roots_hbm), custom_call_target="tpu_custom_call" | custom-call | tf_op jit(solution)/shard_map/ambiguity/pallas_call | solution.py:486
  45.3 1.9 %copy.9 = f32[4,16,16,128]{3,2,1,0:T(8,128)} copy(f32[4,16,16,128]{3,2,1,0:T(8,128)} %ambiguity.1) | data formatting | bytes 1048576

commit v6 on v5

--- a/solution.py
+++ b/solution.py
@@ -287,12 +287,6 @@
         )
 
     def second(k):
-        across(k).wait_recv()
-        for z in range(4):
-            total = outbox[k, 0, z, my_x].astype(F32) + in_x[k, z].astype(F32)
-            sum_x[k, z] = total.astype(BF16)
-        for dz in range(1, 4):
-            around_last(k, dz).start()
         for dz in range(1, 4):
             around(k, dz).wait_recv()
         for side in range(2):
@@ -301,6 +295,12 @@
                 total = total + in_z[k, dz, side].astype(F32)
             sum_z[k, side] = total.astype(BF16)
         across_last(k).start()
+        across(k).wait_recv()
+        for z in range(4):
+            total = outbox[k, 0, z, my_x].astype(F32) + in_x[k, z].astype(F32)
+            sum_x[k, z] = total.astype(BF16)
+        for dz in range(1, 4):
+            around_last(k, dz).start()
 
     def straight(half, o):
         peer = lax.rem(my_seg + o, SEG)
@@ -397,7 +397,9 @@
             else:
                 table[DOPPLER:, (c - 2) * LANES : (c - 1) * LANES] = -piece
 
-        def beams(half, _):
+        def beams(step, _):
+            half = 1 - step
+
             def column(ref, b):
                 at = half * 8 * BLOCKS + b
                 even = ref[pl.ds(at, LANES, stride=8), :].astype(BF16)

time: 47.5 us -> 47.7 us (level)
  no operation moved by 1% of the time
where the time goes in v6:
time: 47.7 us; the launch traced here: 47.3 us
  Pallas kernels  45.4 us (95%)
  local copies, waits for them, and re-layouts  1.87 us (4%)
    pallas_call x1, Pallas kernels, shards(): pl.pallas_call(main_kernel, in_specs=[smem] * 5 + [hbm] * 2, out_specs=pl...  45.4 us
    unnamed x1, local copies, waits for them, and re-layouts  1.87 us

profile of v6, /device:TPU:0, one launch (start us, length us, event | category | flops | bytes accessed | tf_op | source)
XLA Modules:
  0.0 47.3 jit_solution(15679185282353671915)
XLA Ops:
  0.0 45.4 %ambiguity.1 = f32[4,16,16,128]{3,2,1,0:T(8,128)} custom-call(s32[4]{0:T(128)} %owner.1, s32[4]{0:T(128)} %delay.1, s32[4]{0:T(128)} %doppler.1, bf16[32]{0:T(256)(128)(2,1)} %surv_taps.1, bf16[32]{0:T(256)(128)(2,1)} %ref_taps.1, bf16[2,16,65536]{2,1,0:T(8,128)(2,1)} %bitcast.1, f32[1024,128]{1,0:T(8,128)} %constant.2.clone.roots_hbm), custom_call_target="tpu_custom_call" | custom-call | tf_op jit(solution)/shard_map/ambiguity/pallas_call | solution.py:488
  45.4 1.9 %copy.9 = f32[4,16,16,128]{3,2,1,0:T(8,128)} copy(f32[4,16,16,128]{3,2,1,0:T(8,128)} %ambiguity.1) | data formatting | bytes 1048576

commit v7 on v6

--- a/solution.py
+++ b/solution.py
@@ -170,7 +170,7 @@
             moved = jnp.where(mine, moved, 0.0).astype(BF16)
             ref_in[k, part * 8 : (part + 1) * 8] = moved.reshape(8, 16, LANES)
 
-    groups = ((0, 1), (1, 3))
+    groups = ((0, 1), (1, 1), (2, 2))
 
     def scatter(g, o):
         base, count = groups[g]
@@ -232,13 +232,17 @@
     pl.semaphore_wait(barrier, BEAM - 1 + SEG - 1)
     for o in range(1, BEAM):
         scatter(0, o).start()
-    for k in range(1, TX):
+    pick(1)
+    for o in range(1, BEAM):
+        scatter(1, o).start()
+    for k in range(2, TX):
         pick(k)
     for o in range(1, BEAM):
-        scatter(1, o).start()
+        scatter(2, o).start()
     fetch_roots.wait()
     spread_sums(0)
     spread_sums(1)
+    spread_sums(2)
     arrive(0)
 
     lane = lax.broadcasted_iota(jnp.int32, (16, LANES), 1)
@@ -430,6 +434,10 @@
         def _():
             arrive(1)
 
+        @pl.when(k == 1)
+        def _():
+            arrive(2)
+
         @pl.when(k > 0)
         def _():
             second(k - 1)
@@ -438,7 +446,7 @@
 
     lax.fori_loop(0, TX, transmitter, 0)
 
-    for g in range(2):
+    for g in range(3):
         for o in range(1, BEAM):
             scatter(g, o).wait_send()
             spread(g, o).wait_send()
@@ -515,10 +523,10 @@
             pltpu.VMEM((2, SEG, 8, 16, LANES), BF16),
             dma((STEPS,)),
             dma,
-            dma((2, BEAM)),
-            dma((2, BEAM)),
-            dma((2, BEAM)),
-            dma((2, BEAM)),
+            dma((3, BEAM)),
+            dma((3, BEAM)),
+            dma((3, BEAM)),
+            dma((3, BEAM)),
             dma((TX, 4)),
             dma((TX, 4)),
             dma((TX, 4)),

time: 47.7 us -> 47.3 us (level)
  no operation moved by 1% of the time
where the time goes in v7:
time: 47.3 us; the launch traced here: 47.1 us
  Pallas kernels  45.2 us (96%)
  local copies, waits for them, and re-layouts  1.87 us (4%)
    pallas_call x1, Pallas kernels, shards(): pl.pallas_call(main_kernel, in_specs=[smem] * 5 + [hbm] * 2, out_specs=pl...  45.2 us
    unnamed x1, local copies, waits for them, and re-layouts  1.87 us

profile of v7, /device:TPU:0, one launch (start us, length us, event | category | flops | bytes accessed | tf_op | source)
XLA Modules:
  0.0 47.1 jit_solution(2639623478831950886)
XLA Ops:
  0.0 45.2 %ambiguity.1 = f32[4,16,16,128]{3,2,1,0:T(8,128)} custom-call(s32[4]{0:T(128)} %owner.1, s32[4]{0:T(128)} %delay.1, s32[4]{0:T(128)} %doppler.1, bf16[32]{0:T(256)(128)(2,1)} %surv_taps.1, bf16[32]{0:T(256)(128)(2,1)} %ref_taps.1, bf16[2,16,65536]{2,1,0:T(8,128)(2,1)} %bitcast.1, f32[1024,128]{1,0:T(8,128)} %constant.2.clone.roots_hbm), custom_call_target="tpu_custom_call" | custom-call | tf_op jit(solution)/shard_map/ambiguity/pallas_call | solution.py:496
  45.2 1.9 %copy.9 = f32[4,16,16,128]{3,2,1,0:T(8,128)} copy(f32[4,16,16,128]{3,2,1,0:T(8,128)} %ambiguity.1) | data formatting | bytes 1048576
